TPU v7x, 32 devices: a whole 2x2x4 slice. The times are simulated.
32 devices in a mesh: row: 8 (over y, x, core), col: 4 (over z).
Axes of the slice: x: 2, y: 2, z: 4, core: 2. Of those that a mesh axis runs over, the one named last changes fastest.
Arguments:
- row_geometry: float32 [4, 8, 16, 4, 2, 256], P('col', 'row'), may hold values from 0 to 1, as said below
- column_geometry: float32 [4, 2, 512], replicated, may hold values from 0 to 1
- octree_slot: int32 [4, 8, 8, 2], P('col'), may hold values from 0 to 15, as said below
- pivots: int32 [256], replicated, may hold values from 0 to 65535, as said below
- lower_inv: float32 [256, 256], replicated, as said below
- upper_inv: float32 [256, 256], replicated, as said below
Outputs:
- slab_out: float32 [8, 4, 8, 256, 512], P('row', 'col')
- upper_block: float32 [256, 256], replicated
Inputs may be any that keep to these rules, and one draw needn't show every extreme that they name: For each process column q and owner d, the entries octree_slot[q, :, d, :] are each local tile number 0 to 15 once. pivots[i] lies between i and 65535. `row_geometry`: the two tiles of one tile row carry equal row geometry in their slots. `lower_inv`: unit lower triangular. `upper_inv`: upper triangular with positive diagonal.
All inputs are finite; a program needn't handle non-finite values.
Results may differ from a plain program's by a relative error of at most 0.0003.
Values sent between devices are 32-bit elements; how exact they have to be, the bound alone decides.
No kernel may reach another device: no remote copies, remote signals or barrier semaphores. Data moves between devices by JAX's collectives and lax.ppermute only.
A program may use at most 64 MiB of HBM per device.

v0:
```python
import jax
import jax.numpy as jnp
from jax import lax
from jax.sharding import PartitionSpec as P

KAPPA = 9.0
SOFTEN = 0.05


def kernel_entries(row_points, column_points):
    quad_count = row_points.shape[-2]
    accumulated = None
    for row_point in range(quad_count):
        for column_point in range(quad_count):
            along_x = (
                row_points[..., 0, row_point, :, None]
                - column_points[..., 0, column_point, None, :]
            )
            along_y = (
                row_points[..., 1, row_point, :, None]
                - column_points[..., 1, column_point, None, :]
            )
            along_z = (
                row_points[..., 2, row_point, :, None]
                - column_points[..., 2, column_point, None, :]
            )
            spacing = jnp.sqrt(along_x * along_x + along_y * along_y + along_z * along_z)
            summand = (
                row_points[..., 3, row_point, :, None]
                * column_points[..., 3, column_point, None, :]
                * jnp.cos(KAPPA * spacing)
                / (spacing + SOFTEN)
            )
            accumulated = summand if accumulated is None else accumulated + summand
    return accumulated


def tracked_swaps(pivots):
    tile_size = pivots.shape[0]
    positions = jnp.concatenate([jnp.arange(tile_size, dtype=jnp.int32), pivots])
    same = positions[:, None] == positions[None, :]
    first_slot = jnp.argmax(same, axis=1)

    def advance(index_now, compact):
        slot_here = first_slot[index_now]
        slot_there = first_slot[index_now + tile_size]
        at_step = compact[slot_here]
        at_target = compact[slot_there]
        return compact.at[slot_here].set(at_target).at[slot_there].set(at_step)

    compact = lax.fori_loop(0, tile_size, advance, positions)
    values = jnp.take(compact, first_slot, axis=0)
    return (positions, values)


def per_device(row_geometry, column_geometry, octree_slot, pivots, lower_inv, upper_inv):
    row_count = lax.axis_size("row")
    col_count = lax.axis_size("col")
    row_place = lax.axis_index("row")
    col_place = lax.axis_index("col")
    tile_size = pivots.shape[0]
    slots_all = row_geometry.shape[2]
    tile_rows_dev = slots_all // 2
    quad_count = row_geometry.shape[4]
    fill_geometry = row_geometry[0, 0]
    slot_table = octree_slot[0]
    fill_tiles = lax.dynamic_index_in_dim(slot_table, row_place, 0, keepdims=False).reshape(-1)
    arrival = lax.dynamic_index_in_dim(slot_table, row_place, 1, keepdims=False).reshape(-1)
    placement_index = (
        jnp.zeros((slots_all,), jnp.int32).at[arrival].set(jnp.arange(slots_all, dtype=jnp.int32))
    )
    column_halves = column_geometry.reshape(4, quad_count, 2, tile_size)
    halves = jnp.take(column_halves, fill_tiles % 2, axis=2)
    filled = kernel_entries(fill_geometry, jnp.transpose(halves, (2, 0, 1, 3)))
    arrived = lax.all_to_all(filled, "row", split_axis=0, concat_axis=0, tiled=True)
    owned_tiles = jnp.take(arrived, placement_index, axis=0)
    slab_rows = (
        owned_tiles.reshape(tile_rows_dev, 2, tile_size, tile_size)
        .transpose(0, 2, 1, 3)
        .reshape(tile_rows_dev * tile_size, 2 * tile_size)
    )
    positions, values = tracked_swaps(pivots)
    local_tile_rows = row_place + row_count * (
        col_place + col_count * jnp.arange(tile_rows_dev, dtype=jnp.int32)
    )
    global_rows = (
        local_tile_rows[:, None] * tile_size + jnp.arange(tile_size, dtype=jnp.int32)[None, :]
    ).reshape(-1)
    matched = global_rows[:, None] == positions[None, :]
    found = jnp.max(jnp.where(matched, values[None, :], -1), axis=1)
    sources = jnp.where(found >= 0, found, global_rows)
    pivot_sources = values[:tile_size]
    source_tiles = pivot_sources // tile_size
    holds_row = (source_tiles % row_count == row_place) & (
        source_tiles // row_count % col_count == col_place
    )
    local_index = jnp.where(
        holds_row,
        source_tiles // (row_count * col_count) * tile_size + pivot_sources % tile_size,
        0,
    )
    pivot_part = jnp.where(holds_row[:, None], jnp.take(slab_rows, local_index, axis=0), 0.0)
    leading = (row_place == 0) & (col_place == 0)
    initial_part = jnp.where(leading, slab_rows[:tile_size], 0.0)
    initial_top, pivot_top = lax.psum((initial_part, pivot_part), ("row", "col"))
    from_pivots = jnp.take(pivot_top, jnp.minimum(global_rows, tile_size - 1), axis=0)
    from_initial = jnp.take(initial_top, jnp.minimum(sources, tile_size - 1), axis=0)
    permuted = jnp.where(
        (global_rows < tile_size)[:, None],
        from_pivots,
        jnp.where((sources == global_rows)[:, None], slab_rows, from_initial),
    )
    highest = lax.Precision.HIGHEST
    upper_block = jnp.dot(
        lower_inv, pivot_top[:, tile_size:], precision=highest, preferred_element_type=jnp.float32
    )
    lower_panel = jnp.dot(
        permuted[:, :tile_size], upper_inv, precision=highest, preferred_element_type=jnp.float32
    )
    trailing = permuted[:, tile_size:] - jnp.dot(
        lower_panel, upper_block, precision=highest, preferred_element_type=jnp.float32
    )
    slab_out = jnp.concatenate([lower_panel, trailing], axis=1).reshape(
        1, 1, tile_rows_dev, tile_size, 2 * tile_size
    )
    return (slab_out, upper_block)


def solution(mesh):
    placed = (
        P("col", "row", None, None, None, None),
        P(),
        P("col", None, None, None),
        P(),
        P(),
        P(),
    )
    return jax.shard_map(
        per_device,
        mesh=mesh,
        in_specs=placed,
        out_specs=(P("row", "col", None, None, None), P()),
        check_vma=False,
    )
```

profile of v0, /device:TPU:0, one launch (start us, length us, event | category | flops | bytes accessed | tf_op | source)
XLA Modules:
  0.0 1934.2 jit_solution(667069928864595273)
XLA Ops:
  8.2 1.0 dynamic-slice_reduce_fusion
  10.9 1.0 fusion.17
  12.0 153.8 %divide_add_fusion = f32[16,256,256]{2,1,0:T(8,128)} fusion(f32[16,256]{1,0:T(8,128)S(1)} %get-tuple-element.183, f32[16,256]{1,0:T(8,128)S(1)} %get-tuple-element.184, f32[16,256]{1,0:T(8,128)S(1)} %get-tuple-element.185, f32[16,256]{1,0:T(8,128)S(1)} %get-tuple-element.186, f32[16,256]{1,0:T(8,128)S(1)} %bitcast.101, f32[16,256]{1,0:T(8,128)S(1)} %bitcast.95, ...), kind=kLoop, calls=%fused_computation.14 | loop fusion | flops 57671680 | bytes 4456448 | tf_op jit(solution)/shard_map/add | solution.py:34
  165.8 5.3 all-to-all-start
  173.3 1534.3 %while.17 = (s32[]{:T(128)}, s32[512]{0:T(512)S(1)}, s32[512]{0:T(512)S(1)}, s32[]{:T(128)}, s32[]{:T(128)}, /*index=5*/s32[]{:T(128)}, s32[]{:T(128)}, s32[]{:T(128)}, s32[]{:T(128)}) while((s32[]{:T(128)}, s32[512]{0:T(512)S(1)}, s32[512]{0:T(512)S(1)}, s32[]{:T(128)}, s32[]{:T(128)}, /*index=5*/s32[]{:T(128)}, s32[]{:T(128)}, s32[]{:T(128)}, ...), condition=%wide.region_2.3_spmd, body=%wide.region_1.2_spmd.sunk | while | flops 20 | bytes 2363 | solution.py:51
  1707.5 3.5 gather_fusion
  1711.1 5.0 gather_fusion.2
  1716.2 4.7 select_bitcast_fusion
  1720.8 5.5 copy.39
  1726.4 1.1 slice_select_fusion
  1727.4 6.2 copy.64
  1734.8 5.3 copy.40
  1740.2 3.4 gather_fusion.3
  1745.5 132.6 %all-reduce.3.cloned.1.call-done = (f32[256,512]{1,0:T(8,128)}, f32[256,512]{1,0:T(8,128)}) async-done(((f32[256,512]{1,0:T(8,128)}, f32[256,512]{1,0:T(8,128)}), (f32[256,512]{1,0:T(8,128)}, f32[256,512]{1,0:T(8,128)})) %all-reduce.3.cloned.1.call-update) | async-done | bytes 1048592 | tf_op jit(solution)/shard_map/psum | solution.py:105
  1878.2 1.6 fusion.3
  1880.6 8.9 gather_fusion.4
  1889.5 5.4 copy.41
  1895.0 8.9 gather_fusion.5
  1903.9 5.4 copy.43
  1909.4 6.1 fusion
  1915.5 2.0 fusion.1
  1917.5 2.0 convolution_subtract_fusion
  1919.6 2.4 pad_maximum_fusion
  1922.0 5.3 copy.46
  (1087 shorter events, 676.4 us)
Async XLA Ops:
  7.2 1908.3 %copy-start = (f32[256,256]{1,0:T(8,128)S(1)}, f32[256,256]{1,0:T(8,128)}, u32[]{:S(2)}) copy-start(f32[256,256]{1,0:T(8,128)} %param.19) | copy-start | bytes 786436
  165.8 5.4 copy-start.4
  165.8 1545.3 %all-to-all-start = ((f32[16,256,256]{2,1,0:T(8,128)}), f32[16,256,256]{2,1,0:T(8,128)}, u32[]{:S(2)}, u32[]{:S(2)}) async-start(f32[16,256,256]{2,1,0:T(8,128)} %divide_add_fusion), calls=%async_computation | async-start | bytes 8388608 | tf_op jit(solution)/shard_map/all_to_all | solution.py:75
  171.2 1707.0 %all-reduce.3.cloned.1.call-start = ((), (), s32[]{:S(2)}) async-start(), calls=%async_computation.1 | async-start | bytes 2097152 | tf_op jit(solution)/shard_map/psum | solution.py:105
  1740.2 138.0 %copy-start.3 = (f32[256,256]{1,0:T(8,128)S(1)}, f32[256,256]{1,0:T(8,128)}, u32[]{:S(2)}) copy-start(f32[256,256]{1,0:T(8,128)} %param.18) | copy-start | bytes 786436
  1878.2 2.5 copy-start.1
  1889.5 5.5 copy-start.2
Sparse Core Ops, SparseCore 0:
  1744.7 133.3 all-reduce.2
where the time goes:
time: 1950 us; the launch traced here: 1930 us
  loops' own time  867 us (44%)
  other arithmetic  542 us (28%)
  local copies, waits for them, and re-layouts  367 us (19%)
  waiting for transfers between devices  133 us (7%)
    another operation x1, loops' own time, tracked_swaps(): compact = lax.fori_loop(0, tile_size, advance, positions)  867 us
    scatter x512, other arithmetic, advance(): return compact.at[slot_here].set(at_target).at[slot_there].set(at_step)  371 us
    add x1, other arithmetic, kernel_entries(): accumulated = summand if accumulated is None else accumulated + summand  154 us
    dynamic_slice x256, local copies, waits for them, and re-layouts, advance(): slot_there = first_slot[index_now + tile_size]  148 us
    another operation x256, local copies, waits for them, and re-layouts  148 us
    psum x1, waiting for transfers between devices, per_device(): lax.psum((initial_part, pivot_part), ('row', 'col'))  133 us
  transfers between devices with their start and end apart: 2, of which 1 were waited for; matrix products, arithmetic and copies ran while one was open for 35% of the time, Pallas kernels for 0%

commit v1 on v0

v1 whole, which is shorter than its diff:
```python
import functools
import math

import jax
import jax.numpy as jnp
from jax import lax
from jax.experimental import pallas as pl
from jax.experimental.pallas import tpu as pltpu
from jax.sharding import PartitionSpec as P

KAPPA = 9.0
SOFTEN = 0.05
HIGHEST = lax.Precision.HIGHEST

FIT = (1.99999988, -4.38646535, 1.60268206, -0.22763882)
LEAD = FIT[3]
A0, A1, A2 = FIT[0] / LEAD, FIT[1] / LEAD, FIT[2] / LEAD
TRIPLE = 3.0 / (LEAD * LEAD)
TURNS = KAPPA / (2.0 * math.pi)
SOFT_TURNS = SOFTEN * TURNS
WEIGHT = 0.5 * LEAD**3 * TURNS


def split(value, divisor):
    if divisor & (divisor - 1) == 0:
        shift = divisor.bit_length() - 1
        return lax.shift_right_logical(value, shift), value & (divisor - 1)
    return lax.div(value, divisor), lax.rem(value, divisor)


def as_column(row):
    count = row.shape[1]
    return jnp.transpose(jnp.broadcast_to(row, (8, count)))[:, :1]


def exact_dot(left, right):
    return jnp.dot(left, right, precision=HIGHEST, preferred_element_type=jnp.float32)


def pivot_place(pivots, tile, row_count, col_count):
    tiles, lanes = split(pivots, tile)
    rest, owner_row = split(tiles, row_count)
    local, owner_col = split(rest, col_count)
    return owner_row, owner_col, local, lanes


def pack_kernel(sizes, geometry, table, pivots, out, flat):
    row_count, col_count, tile, comps, slots = sizes
    me_row = lax.axis_index("row")
    me_col = lax.axis_index("col")
    quad = geometry.shape[2]
    for slot in range(row_count * slots):
        for axis in range(comps // quad):
            flat[pl.ds(slot * comps + axis * quad, quad), :] = geometry[slot, axis]
    piv = pivots[...]
    owner_row, owner_col, local, lanes = pivot_place(piv, tile, row_count, col_count)
    picker = (lax.broadcasted_iota(jnp.int32, (tile, tile), 0) == lanes).astype(jnp.float32)
    picked = exact_dot(flat[...], picker)
    top = jnp.zeros((comps, tile), jnp.float32)
    chosen = jnp.zeros((comps, tile), jnp.float32)
    for owner in range(row_count):
        for s in range(slots):
            number = table[me_row, owner, s]
            rows = (owner * slots + s) * comps
            block = flat[pl.ds(rows, comps), :]
            out[owner, pl.ds(s * comps, comps), :] = block
            hit = (owner_col == me_col) & (owner_row == owner) & (2 * local == number)
            chosen = jnp.where(hit, picked[rows : rows + comps], chosen)
            if owner == 0:
                here = jnp.full((comps, tile), (number == 0) & (me_col == 0))
                top = jnp.where(here, block, top)
    for owner in range(row_count):
        out[owner, pl.ds(slots * comps, comps), :] = top
        out[owner, pl.ds((slots + 1) * comps, comps), :] = chosen


def entries(rows, columns):
    total = None
    for column in columns:
        partial = None
        for row in rows:
            along_x = row[0] - column[0]
            along_y = row[1] - column[1]
            along_z = row[2] - column[2]
            square = along_x * along_x + along_y * along_y + along_z * along_z
            spacing = 1.0 / lax.rsqrt(square)
            scale = 1.0 / (spacing + SOFT_TURNS)
            turn = spacing - jnp.round(spacing)
            v = turn * turn
            c = ((v + A2) * v + A1) * v + A0
            value = (c * (c * c - TRIPLE)) * scale * row[3]
            partial = value if partial is None else partial + value
        partial = partial * column[3]
        total = partial if total is None else total + partial
    return total


def fill(points, base, columns, chunks, target, target_base, quad, height):
    for group in range(height // 8):
        block = points[pl.ds(base + group * 8, 8), :]
        rows = [
            [
                jnp.broadcast_to(block[:, axis * quad + a : axis * quad + a + 1], (8, 128))
                for axis in range(4)
            ]
            for a in range(quad)
        ]
        for place, chunk in enumerate(chunks):
            cols = [[columns[axis * quad + b, chunk] for axis in range(4)] for b in range(quad)]
            target[pl.ds(target_base + group * 8, 8), pl.ds(place * 128, 128)] = entries(rows, cols)


def main_kernel(
    sizes, arrived, shared, table, pivots, column_geometry, lower_inv, upper_inv,
    slab, upper_block, columns, owned, points, top_points, filled, right_high, right_low,
):
    row_count, col_count, tile, comps, slots = sizes
    quad = column_geometry.shape[1]
    me_row = lax.axis_index("row")
    me_col = lax.axis_index("col")
    t = pl.program_id(0)
    tile_rows = pl.num_programs(0)
    lane_chunks = tile // 128
    height = 16

    @pl.when(t == 0)
    def _():
        scale = [TURNS] * (3 * quad) + [WEIGHT] * quad
        for axis in range(4):
            for b in range(quad):
                for chunk in range(2 * lane_chunks):
                    part = column_geometry[axis, pl.ds(b, 1), pl.ds(chunk * 128, 128)]
                    if axis < 3:
                        part = part * TURNS
                    columns[axis * quad + b, chunk] = jnp.broadcast_to(part, (8, 128))
        for source in range(row_count):
            for s in range(slots):
                number = table[source, me_row, s]

                @pl.when(number & 1 == 0)
                def _():
                    owned[lax.shift_right_logical(number, 1)] = arrived[source, pl.ds(s * comps, comps), :]

        piv = pivots[...]
        piv_col = as_column(piv)
        owner_row, owner_col, local, lanes = pivot_place(piv, tile, row_count, col_count)
        down = lax.broadcasted_iota(jnp.int32, (tile, tile), 0)
        across = lax.broadcasted_iota(jnp.int32, (tile, tile), 1)
        same = piv_col == piv
        earlier = down < across
        line = lax.broadcasted_iota(jnp.int32, (1, tile), 1)
        before = jnp.max(jnp.where(same & earlier, down, -1), axis=0, keepdims=True)
        after = jnp.max(jnp.where(same & (down > across), 1, 0), axis=0, keepdims=True)
        parent = jnp.max(jnp.where((piv_col == across) & earlier, down, -1), axis=0, keepdims=True)
        moved = jnp.max(parent)
        root = jnp.where(parent >= 0, parent, line)

        def doubled(carry):
            _, now = carry
            pick = (down == now).astype(jnp.float32)
            new = jnp.dot(
                jnp.broadcast_to(now, (8, tile)).astype(jnp.float32), pick,
                precision=HIGHEST, preferred_element_type=jnp.float32,
            )[:1].astype(jnp.int32)
            return jnp.max(jnp.where(new != now, 1, 0)), new

        _, root = lax.while_loop(lambda carry: carry[0] > 0, doubled, (jnp.where(moved >= 0, 1, 0), root))

        top = shared[pl.ds(0, comps), :]
        chosen = shared[pl.ds(comps, comps), :]
        carried = exact_dot(top, (down == root).astype(jnp.float32))
        again = exact_dot(carried, (down == before).astype(jnp.float32))
        new_top = jnp.where(before >= 0, again, chosen)
        mine = (owner_row == me_row) & (owner_col == me_col) & (after == 0) & (piv >= tile)
        lane_col = as_column(lanes)
        place = (lane_col == across).astype(jnp.float32)
        parts = []
        for k in range(owned.shape[0]):
            parts.append(jnp.where(mine & (local == k), carried, 0.0))
        for k in range(owned.shape[0]):
            parts.append(jnp.broadcast_to(jnp.where(mine & (local == k), 1.0, 0.0), (8, tile)))
        sent = exact_dot(jnp.concatenate(parts, axis=0), place)
        factor = jnp.where(
            lax.broadcasted_iota(jnp.int32, (comps, tile), 0) < 3 * quad, TURNS, WEIGHT
        )
        leading = jnp.full((comps, tile), (me_row == 0) & (me_col == 0))
        count = owned.shape[0]
        for k in range(count):
            fresh = sent[k * comps : (k + 1) * comps]
            hit = sent[(count * comps + k * 8) : (count * comps + k * 8 + comps)] > 0.5
            mixed = jnp.where(hit, fresh, owned[k])
            if k == 0:
                mixed = jnp.where(leading, new_top, mixed)
            points[k] = jnp.transpose(mixed * factor)
        top_points[...] = jnp.transpose(new_top * factor)

        def top_step(step, carry):
            base = pl.multiple_of(step * height, height)
            fill(top_points, base, columns, range(lane_chunks, 2 * lane_chunks), filled, base, quad, height)
            return carry

        lax.fori_loop(0, tile // height, top_step, 0)
        upper = exact_dot(lower_inv[...], filled[:, :tile])
        upper_block[...] = upper
        both = jnp.concatenate([upper_inv[...], -exact_dot(upper_inv[...], upper)], axis=1)
        high = both.astype(jnp.bfloat16)
        right_high[...] = high
        right_low[...] = (both - high.astype(jnp.float32)).astype(jnp.bfloat16)

    def step(index, carry):
        base = pl.multiple_of(index * height, height)
        fill(points.at[t], base, columns, range(2 * lane_chunks), filled, base, quad, height)
        return carry

    lax.fori_loop(0, tile // height, step, 0)
    left = filled[:, :tile]
    high = left.astype(jnp.bfloat16)
    low = (left - high.astype(jnp.float32)).astype(jnp.bfloat16)
    dot = functools.partial(jnp.dot, preferred_element_type=jnp.float32)
    product = dot(high, right_low[...]) + dot(low, right_high[...]) + dot(high, right_high[...])
    slab[:, :tile] = product[:, :tile]
    slab[:, tile:] = product[:, tile:] + filled[:, tile:]


def per_device(row_geometry, column_geometry, octree_slot, pivots, lower_inv, upper_inv):
    row_count = lax.axis_size("row")
    col_count = lax.axis_size("col")
    tile = pivots.shape[0]
    slots_all, axes, quad = row_geometry.shape[2:5]
    slots = slots_all // row_count
    tile_rows = slots_all // 2
    comps = axes * quad
    sizes = (row_count, col_count, tile, comps, slots)
    geometry = row_geometry[0, 0]
    table = octree_slot[0]
    pivot_row = pivots.reshape(1, tile)
    vmem = pl.BlockSpec(memory_space=pltpu.VMEM)
    smem = pl.BlockSpec(memory_space=pltpu.SMEM)
    depth = (slots + 2) * comps
    packed = pl.pallas_call(
        functools.partial(pack_kernel, sizes),
        out_shape=jax.ShapeDtypeStruct((row_count, depth, tile), jnp.float32),
        in_specs=[vmem, smem, vmem],
        out_specs=vmem,
        scratch_shapes=[pltpu.VMEM((slots_all * comps, tile), jnp.float32)],
        name="pack",
    )(geometry, table, pivot_row)
    arrived = lax.all_to_all(packed, "row", 0, 0, tiled=True)
    shared = jnp.sum(arrived[:, slots * comps :, :], axis=0)
    step = 1
    while step < col_count:
        partner = [(j, j ^ step) for j in range(col_count)]
        shared = shared + lax.ppermute(shared, "col", partner)
        step *= 2
    slab, upper_block = pl.pallas_call(
        functools.partial(main_kernel, sizes),
        grid=(tile_rows,),
        out_shape=(
            jax.ShapeDtypeStruct((tile_rows * tile, 2 * tile), jnp.float32),
            jax.ShapeDtypeStruct((tile, tile), jnp.float32),
        ),
        in_specs=[vmem, vmem, smem, vmem, vmem, vmem, vmem],
        out_specs=(
            pl.BlockSpec((tile, 2 * tile), lambda t: (t, 0)),
            pl.BlockSpec((tile, tile), lambda t: (0, 0)),
        ),
        scratch_shapes=[
            pltpu.VMEM((comps, 2 * tile // 128, 8, 128), jnp.float32),
            pltpu.VMEM((tile_rows, comps, tile), jnp.float32),
            pltpu.VMEM((tile_rows, tile, comps), jnp.float32),
            pltpu.VMEM((tile, comps), jnp.float32),
            pltpu.VMEM((tile, 2 * tile), jnp.float32),
            pltpu.VMEM((tile, 2 * tile), jnp.bfloat16),
            pltpu.VMEM((tile, 2 * tile), jnp.bfloat16),
        ],
        name="panel",
    )(arrived, shared, table, pivot_row, column_geometry, lower_inv, upper_inv)
    return (slab.reshape(1, 1, tile_rows, tile, 2 * tile), upper_block)


def solution(mesh):
    placed = (
        P("col", "row", None, None, None, None),
        P(),
        P("col", None, None, None),
        P(),
        P(),
        P(),
    )
    return jax.shard_map(
        per_device,
        mesh=mesh,
        in_specs=placed,
        out_specs=(P("row", "col", None, None, None), P()),
        check_vma=False,
    )
```

time: 1950 us -> 61.1 us (0.03)
  loops' own time: 867 us -> 0 us
  other arithmetic: 542 us -> 0.62 us
  local copies, waits for them, and re-layouts: 367 us -> 1.42 us
  waiting for transfers between devices: 133 us -> 4.21 us
  Pallas kernels: 0 us -> 37.4 us
    another operation x1 -> x0, loops' own time: 867 us -> none  [tracked_swaps(): compact = lax.fori_loop(0, tile_size, advance, positions)]
    scatter x512 -> x0, other arithmetic: 371 us -> none  [advance(): return compact.at[slot_here].set(at_target).at[slot_there].set(at_step)]
    add x1 -> x2, other arithmetic: 154 us -> 0.61 us  [per_device(): shared = shared + lax.ppermute(shared, 'col', partner)]
    dynamic_slice x259 -> x0, local copies, waits for them, and re-layouts: 150 us -> none  [the longest x256 148 us: advance(): slot_there = first_slot[index_now + tile_size]]
    another operation x256 -> x0, local copies, waits for them, and re-layouts: 148 us -> none
    psum x1 -> x0, waiting for transfers between devices: 133 us -> none  [per_device(): lax.psum((initial_part, pivot_part), ('row', 'col'))]
    gather x8 -> x0, local copies, waits for them, and re-layouts: 41.3 us -> none  [the longest x2 14.4 us: per_device(): jnp.take(pivot_top, jnp.minimum(global_rows, tile_size - 1), axis=0)]
    pallas_call x0 -> x2, Pallas kernels: none -> 37.4 us  [the longest x1 35 us: per_device(): pl.pallas_call(functools.partial(main_kernel, sizes), grid=(tile_rows,),...]
  transfers between devices with their start and end apart: 2 -> 2, of which waited for: 1 -> 2; matrix products, arithmetic and copies ran while one was open for 35% -> 0% of each run, Pallas kernels for 0% -> 0%
where the time goes in v1:
time: 61.1 us; the launch traced here: 60.6 us
  Pallas kernels  37.4 us (61%)
  blocking collectives  12.1 us (20%)
  starting transfers between devices  4.23 us (7%)
  waiting for transfers between devices  4.21 us (7%)
  local copies, waits for them, and re-layouts  1.42 us (2%)
  between operations  0.64 us (1%)
  other arithmetic  0.62 us (1%)
    pallas_call x1, Pallas kernels, per_device(): pl.pallas_call(functools.partial(main_kernel, sizes), grid=(tile_rows,),...  35 us
    all_to_all x1, blocking collectives, per_device(): arrived = lax.all_to_all(packed, 'row', 0, 0, tiled=True)  12.1 us
    ppermute x2, starting transfers between devices, per_device(): shared = shared + lax.ppermute(shared, 'col', partner)  4.23 us
    ppermute x2, waiting for transfers between devices, per_device(): shared = shared + lax.ppermute(shared, 'col', partner)  4.21 us
    pallas_call x1, Pallas kernels, per_device(): pl.pallas_call(functools.partial(pack_kernel, sizes), out_shape=jax.Shape...  2.39 us
    squeeze x1, local copies, waits for them, and re-layouts, per_device(): table = octree_slot[0]  1.41 us
  transfers between devices with their start and end apart: 2, of which 2 were waited for; matrix products, arithmetic and copies ran while one was open for 0% of the time, Pallas kernels for 0%

profile of v1, /device:TPU:0, one launch (start us, length us, event | category | flops | bytes accessed | tf_op | source)
XLA Modules:
  0.0 60.6 jit_solution(5648510326523352018)
XLA Ops:
  0.6 1.4 %copy.9.table = s32[8,8,2]{2,1,0:T(8,128)} copy(s32[8,8,2]{1,2,0:T(2,128)} %bitcast.5) | data formatting | bytes 1024 | tf_op jit(solution)/shard_map/squeeze | solution.py:235
  2.0 2.4 %pack.1 = f32[8,32,256]{2,1,0:T(8,128)} custom-call(f32[16,4,2,256]{3,2,1,0:T(2,128)} %bitcast.4, s32[8,8,2]{2,1,0:T(8,128)} %copy.9.table, s32[1,256]{1,0:T(1,128)} %bitcast.6), custom_call_target="tpu_custom_call" | custom-call | tf_op jit(solution)/shard_map/pack/pallas_call | solution.py:240
  4.4 12.1 %all_to_all.5.arrived = f32[8,32,256]{2,1,0:T(8,128)S(1)} all-to-all(f32[8,32,256]{2,1,0:T(8,128)} %pack.1), channel_id=1, replica_groups=mesh['row'=8,'col'=4] {'row'}, dimensions={0} | all-to-all | bytes 524288 | tf_op jit(solution)/shard_map/all_to_all | solution.py:248
  16.5 0.0 copy-start
  16.5 1.6 %collective-permute-start = (f32[16,256]{1,0:T(8,128)S(1)}, f32[16,256]{1,0:T(8,128)S(1)}, u32[]{:S(2)}, u32[]{:S(2)}) collective-permute-start(f32[16,256]{1,0:T(8,128)S(1)} %slice_reduce_fusion), channel_id=1, source_target_pairs={{0,1},{1,0},{2,3},{3,2},{4,5},{5,4},{6,7},{7,6},{8,9},{9,8},{10,11... | collective-permute-start | bytes 49160 | tf_op jit(solution)/shard_map/ppermute | solution.py:253
  18.2 2.2 %collective-permute-done = f32[16,256]{1,0:T(8,128)S(1)} collective-permute-done((f32[16,256]{1,0:T(8,128)S(1)}, f32[16,256]{1,0:T(8,128)S(1)}, u32[]{:S(2)}, u32[]{:S(2)}) %collective-permute-start) | collective-permute-done | bytes 16416 | tf_op jit(solution)/shard_map/ppermute | solution.py:253
  20.4 2.6 %collective-permute-start.1 = (f32[16,256]{1,0:T(8,128)S(1)}, f32[16,256]{1,0:T(8,128)S(1)}, u32[]{:S(2)}, u32[]{:S(2)}) collective-permute-start(f32[16,256]{1,0:T(8,128)S(1)} %add.6), channel_id=1, source_target_pairs={{0,2},{1,3},{2,0},{3,1},{4,6},{5,7},{6,4},{7,5},{8,10},{9,11},{10,... | collective-permute-start | bytes 49160 | tf_op jit(solution)/shard_map/ppermute | solution.py:253
  22.9 2.0 %collective-permute-done.1 = f32[16,256]{1,0:T(8,128)S(1)} collective-permute-done((f32[16,256]{1,0:T(8,128)S(1)}, f32[16,256]{1,0:T(8,128)S(1)}, u32[]{:S(2)}, u32[]{:S(2)}) %collective-permute-start.1) | collective-permute-done | bytes 16416 | tf_op jit(solution)/shard_map/ppermute | solution.py:253
  25.0 0.6 add.7.shared
  25.6 0.0 copy-done
  25.6 35.0 %panel.1 = (f32[2048,512]{1,0:T(8,128)}, f32[256,256]{1,0:T(8,128)}) custom-call(f32[8,32,256]{2,1,0:T(8,128)} %copy-done, f32[16,256]{1,0:T(8,128)} %add.7.shared, s32[8,8,2]{2,1,0:T(8,128)} %copy.9.table, s32[1,256]{1,0:T(1,128)} %bitcast.7, f32[4,2,512]{2,1,0:T(2,128)} %column_geometry.1, f32[256,256]{1,0:T(8,128)} %lower_inv.1, f32[256,256]{1,0:T(8,128)} %upper_inv.1), custom_call_target="tpu_custom_call" | custom-call | tf_op jit(solution)/shard_map/panel/pallas_call | solution.py:255
  (2 shorter events, 0.0 us)
Async XLA Ops:
  16.5 9.1 %copy-start = (f32[8,32,256]{2,1,0:T(8,128)}, f32[8,32,256]{2,1,0:T(8,128)S(1)}, u32[]{:S(2)}) copy-start(f32[8,32,256]{2,1,0:T(8,128)S(1)} %all_to_all.5.arrived) | copy-start | bytes 786436
  16.5 3.8 %collective-permute-start = (f32[16,256]{1,0:T(8,128)S(1)}, f32[16,256]{1,0:T(8,128)S(1)}, u32[]{:S(2)}, u32[]{:S(2)}) collective-permute-start(f32[16,256]{1,0:T(8,128)S(1)} %slice_reduce_fusion), channel_id=1, source_target_pairs={{0,1},{1,0},{2,3},{3,2},{4,5},{5,4},{6,7},{7,6},{8,9},{9,8},{10,11... | collective-permute-start | bytes 49160 | tf_op jit(solution)/shard_map/ppermute | solution.py:253
  20.4 4.6 %collective-permute-start.1 = (f32[16,256]{1,0:T(8,128)S(1)}, f32[16,256]{1,0:T(8,128)S(1)}, u32[]{:S(2)}, u32[]{:S(2)}) collective-permute-start(f32[16,256]{1,0:T(8,128)S(1)} %add.6), channel_id=1, source_target_pairs={{0,2},{1,3},{2,0},{3,1},{4,6},{5,7},{6,4},{7,5},{8,10},{9,11},{10,... | collective-permute-start | bytes 49160 | tf_op jit(solution)/shard_map/ppermute | solution.py:253

commit v2 on v1

--- a/solution.py
+++ b/solution.py
@@ -19,6 +19,8 @@
 TURNS = KAPPA / (2.0 * math.pi)
 SOFT_TURNS = SOFTEN * TURNS
 WEIGHT = 0.5 * LEAD**3 * TURNS
+NEAR = (0.007 * TURNS) ** 2
+HEIGHT = 64
 
 
 def split(value, divisor):
@@ -95,6 +97,91 @@
     return total
 
 
+def three_parts(value):
+    parts = []
+    for _ in range(3):
+        part = value.astype(jnp.bfloat16).astype(jnp.float32)
+        parts.append(part)
+        value = value - part
+    return parts
+
+
+def centred(geometry):
+    u = (geometry - 0.5) * TURNS
+    squares = u * u
+    norm = squares + pltpu.roll(squares, 6, 0) + pltpu.roll(squares, 4, 0)
+    return three_parts(u), three_parts(norm)
+
+
+def left_features(geometry):
+    parts, norms = centred(geometry)
+    row = lax.broadcasted_iota(jnp.int32, geometry.shape, 0)
+    stacked = jnp.where(
+        row < 2,
+        norms[0],
+        jnp.where(
+            row < 4,
+            pltpu.roll(norms[1], 2, 0),
+            jnp.where(row < 6, pltpu.roll(norms[2], 4, 0), 0.0),
+        ),
+    )
+    blocks = [parts[i] for i in range(3) for _ in range(3)] + [stacked, jnp.ones_like(stacked)]
+    return jnp.transpose(jnp.concatenate(blocks, axis=0)).astype(jnp.bfloat16)
+
+
+def right_features(geometry, a, b):
+    parts, norms = centred(geometry)
+    row = lax.broadcasted_iota(jnp.int32, geometry.shape, 0)
+    wanted = (row < 6) & ((row & 1) == a)
+    turned = [part if a == b else pltpu.roll(part, (a - b) % 8, 0) for part in parts]
+    doubled = [jnp.where(wanted, -2.0 * part, 0.0) for part in turned]
+    ones = jnp.where(wanted, 1.0, 0.0)
+    placed = jnp.zeros_like(ones)
+    for i, norm in enumerate(norms):
+        placed = jnp.where(row == i, pltpu.roll(norm, (i - b) % 8, 0) if i != b else norm, placed)
+    blocks = [doubled[j] for _ in range(3) for j in range(3)] + [ones, placed]
+    return jnp.concatenate(blocks, axis=0).astype(jnp.bfloat16)
+
+
+def quick_entries(square, weights, column_weights, quad):
+    total = None
+    for b in range(quad):
+        partial = None
+        for a in range(quad):
+            spacing = 1.0 / lax.rsqrt(square(a, b))
+            scale = 1.0 / (spacing + SOFT_TURNS)
+            turn = spacing - jnp.round(spacing)
+            v = turn * turn
+            c = ((v + A2) * v + A1) * v + A0
+            value = (c * (c * c - TRIPLE)) * scale * weights[a]
+            partial = value if partial is None else partial + value
+        partial = partial * column_weights[b]
+        total = partial if total is None else total + partial
+    return total
+
+
+def quick_fill(squares, points, base, columns, chunks, target, target_base, quad, height):
+    nearest = None
+    count = columns.shape[1]
+    for group in range(height // 8):
+        block = points[pl.ds(base + group * 8, 8), :]
+        weights = [
+            jnp.broadcast_to(block[:, 3 * quad + a : 3 * quad + a + 1], (8, 128)) for a in range(quad)
+        ]
+        for place, chunk in enumerate(chunks):
+            loaded = {}
+            for a in range(quad):
+                for b in range(quad):
+                    lane = ((a * quad + b) * count + chunk) * 128
+                    value = squares[pl.ds(group * 8, 8), pl.ds(lane, 128)]
+                    loaded[a, b] = value
+                    nearest = value if nearest is None else jnp.minimum(nearest, value)
+            target[pl.ds(target_base + group * 8, 8), pl.ds(place * 128, 128)] = quick_entries(
+                lambda a, b: loaded[a, b], weights, [columns[3 * quad + b, chunk] for b in range(quad)], quad
+            )
+    return jnp.where(jnp.min(nearest) < NEAR, 1, 0)
+
+
 def fill(points, base, columns, chunks, target, target_base, quad, height):
     for group in range(height // 8):
         block = points[pl.ds(base + group * 8, 8), :]
@@ -112,7 +199,8 @@
 
 def main_kernel(
     sizes, arrived, shared, table, pivots, column_geometry, lower_inv, upper_inv,
-    slab, upper_block, columns, owned, points, top_points, filled, right_high, right_low,
+    slab, upper_block, columns, owned, points, filled, right_high, right_low,
+    column_points, left, right, *squares,
 ):
     row_count, col_count, tile, comps, slots = sizes
     quad = column_geometry.shape[1]
@@ -121,11 +209,53 @@
     t = pl.program_id(0)
     tile_rows = pl.num_programs(0)
     lane_chunks = tile // 128
-    height = 16
+    height = HEIGHT
+    steps = tile // height
+    everything = range(2 * lane_chunks)
+
+    def distances(block, buffer):
+        rows = left[pl.ds(pl.multiple_of(block * height, height), height), :]
+        buffer[...] = jnp.dot(rows, right[...], preferred_element_type=jnp.float32)
+
+    def sweep(tile_index, chunks, last):
+        def again(index):
+            base = pl.multiple_of(index * height, height)
+            for part in range(0, height, 16):
+                fill(points.at[tile_index], base + part, columns, chunks, filled, base + part, quad, 16)
+
+        def checked(index, near):
+            for part in range(2):
+
+                @pl.when(near[part] > 0)
+                def _():
+                    again(index + part)
+
+        def step(pair, near):
+            index = 2 * pair
+            checked(index - 2, near)
+            flat = tile_index * steps + index
+            found = []
+            for part, (ahead, here) in enumerate(((squares[1], squares[0]), (squares[0], squares[1]))):
+                distances(jnp.minimum(flat + 1 + part, last), ahead)
+                base = pl.multiple_of((index + part) * height, height)
+                found.append(
+                    quick_fill(
+                        here, points.at[tile_index], base, columns, chunks, filled, base, quad, height
+                    )
+                )
+            return tuple(found)
+
+        checked(steps - 2, lax.fori_loop(0, steps // 2, step, (0, 0)))
 
     @pl.when(t == 0)
     def _():
-        scale = [TURNS] * (3 * quad) + [WEIGHT] * quad
+        for axis in range(4):
+            column_points[pl.ds(axis * quad, quad), :] = column_geometry[axis]
+        for a in range(quad):
+            for b in range(quad):
+                right[:, pl.ds((a * quad + b) * 2 * tile, 2 * tile)] = right_features(
+                    column_points[...], a, b
+                )
         for axis in range(4):
             for b in range(quad):
                 for chunk in range(2 * lane_chunks):
@@ -192,14 +322,12 @@
             if k == 0:
                 mixed = jnp.where(leading, new_top, mixed)
             points[k] = jnp.transpose(mixed * factor)
-        top_points[...] = jnp.transpose(new_top * factor)
-
-        def top_step(step, carry):
-            base = pl.multiple_of(step * height, height)
-            fill(top_points, base, columns, range(lane_chunks, 2 * lane_chunks), filled, base, quad, height)
-            return carry
-
-        lax.fori_loop(0, tile // height, top_step, 0)
+            left[pl.ds(k * tile, tile), :] = left_features(mixed)
+        points[count] = jnp.transpose(new_top * factor)
+        left[pl.ds(count * tile, tile), :] = left_features(new_top)
+        distances(count * steps, squares[0])
+        sweep(count, range(lane_chunks, 2 * lane_chunks), count * steps + steps - 1)
+        distances(0, squares[0])
         upper = exact_dot(lower_inv[...], filled[:, :tile])
         upper_block[...] = upper
         both = jnp.concatenate([upper_inv[...], -exact_dot(upper_inv[...], upper)], axis=1)
@@ -207,15 +335,10 @@
         right_high[...] = high
         right_low[...] = (both - high.astype(jnp.float32)).astype(jnp.bfloat16)
 
-    def step(index, carry):
-        base = pl.multiple_of(index * height, height)
-        fill(points.at[t], base, columns, range(2 * lane_chunks), filled, base, quad, height)
-        return carry
-
-    lax.fori_loop(0, tile // height, step, 0)
-    left = filled[:, :tile]
-    high = left.astype(jnp.bfloat16)
-    low = (left - high.astype(jnp.float32)).astype(jnp.bfloat16)
+    sweep(t, everything, tile_rows * steps - 1)
+    lead = filled[:, :tile]
+    high = lead.astype(jnp.bfloat16)
+    low = (lead - high.astype(jnp.float32)).astype(jnp.bfloat16)
     dot = functools.partial(jnp.dot, preferred_element_type=jnp.float32)
     product = dot(high, right_low[...]) + dot(low, right_high[...]) + dot(high, right_high[...])
     slab[:, :tile] = product[:, :tile]
@@ -267,11 +390,15 @@
         scratch_shapes=[
             pltpu.VMEM((comps, 2 * tile // 128, 8, 128), jnp.float32),
             pltpu.VMEM((tile_rows, comps, tile), jnp.float32),
-            pltpu.VMEM((tile_rows, tile, comps), jnp.float32),
-            pltpu.VMEM((tile, comps), jnp.float32),
+            pltpu.VMEM((tile_rows + 1, tile, comps), jnp.float32),
             pltpu.VMEM((tile, 2 * tile), jnp.float32),
             pltpu.VMEM((tile, 2 * tile), jnp.bfloat16),
             pltpu.VMEM((tile, 2 * tile), jnp.bfloat16),
+            pltpu.VMEM((comps, 2 * tile), jnp.float32),
+            pltpu.VMEM(((tile_rows + 1) * tile, 11 * comps), jnp.bfloat16),
+            pltpu.VMEM((11 * comps, quad * quad * 2 * tile), jnp.bfloat16),
+            pltpu.VMEM((HEIGHT, quad * quad * 2 * tile), jnp.float32),
+            pltpu.VMEM((HEIGHT, quad * quad * 2 * tile), jnp.float32),
         ],
         name="panel",
     )(arrived, shared, table, pivot_row, column_geometry, lower_inv, upper_inv)

time: 61.1 us -> 55.4 us (0.907)
  Pallas kernels: 37.4 us -> 31.4 us
    pallas_call x1, Pallas kernels: 35 us -> 29 us  [per_device(): pl.pallas_call(functools.partial(main_kernel, sizes), grid=(tile_rows,),...]
where the time goes in v2:
time: 55.4 us; the launch traced here: 54.6 us
  Pallas kernels  31.4 us (57%)
  blocking collectives  12.1 us (22%)
  starting transfers between devices  4.23 us (8%)
  waiting for transfers between devices  4.21 us (8%)
  local copies, waits for them, and re-layouts  1.42 us (3%)
  between operations  0.64 us (1%)
  other arithmetic  0.62 us (1%)
    pallas_call x1, Pallas kernels, per_device(): pl.pallas_call(functools.partial(main_kernel, sizes), grid=(tile_rows,),...  29 us
    all_to_all x1, blocking collectives, per_device(): arrived = lax.all_to_all(packed, 'row', 0, 0, tiled=True)  12.1 us
    ppermute x2, starting transfers between devices, per_device(): shared = shared + lax.ppermute(shared, 'col', partner)  4.23 us
    ppermute x2, waiting for transfers between devices, per_device(): shared = shared + lax.ppermute(shared, 'col', partner)  4.21 us
    pallas_call x1, Pallas kernels, per_device(): pl.pallas_call(functools.partial(pack_kernel, sizes), out_shape=jax.Shape...  2.39 us
    squeeze x1, local copies, waits for them, and re-layouts, per_device(): table = octree_slot[0]  1.41 us
  transfers between devices with their start and end apart: 2, of which 2 were waited for; matrix products, arithmetic and copies ran while one was open for 0% of the time, Pallas kernels for 0%

profile of v2, /device:TPU:0, one launch (start us, length us, event | category | flops | bytes accessed | tf_op | source)
XLA Modules:
  0.0 54.6 jit_solution(5948763580913934259)
XLA Ops:
  0.6 1.4 %copy.9.table = s32[8,8,2]{2,1,0:T(8,128)} copy(s32[8,8,2]{1,2,0:T(2,128)} %bitcast.5) | data formatting | bytes 1024 | tf_op jit(solution)/shard_map/squeeze | solution.py:358
  2.0 2.4 %pack.1 = f32[8,32,256]{2,1,0:T(8,128)} custom-call(f32[16,4,2,256]{3,2,1,0:T(2,128)} %bitcast.4, s32[8,8,2]{2,1,0:T(8,128)} %copy.9.table, s32[1,256]{1,0:T(1,128)} %bitcast.6), custom_call_target="tpu_custom_call" | custom-call | tf_op jit(solution)/shard_map/pack/pallas_call | solution.py:363
  4.4 12.1 %all_to_all.5.arrived = f32[8,32,256]{2,1,0:T(8,128)S(1)} all-to-all(f32[8,32,256]{2,1,0:T(8,128)} %pack.1), channel_id=1, replica_groups=mesh['row'=8,'col'=4] {'row'}, dimensions={0} | all-to-all | bytes 524288 | tf_op jit(solution)/shard_map/all_to_all | solution.py:371
  16.5 0.0 copy-start
  16.5 1.6 %collective-permute-start = (f32[16,256]{1,0:T(8,128)S(1)}, f32[16,256]{1,0:T(8,128)S(1)}, u32[]{:S(2)}, u32[]{:S(2)}) collective-permute-start(f32[16,256]{1,0:T(8,128)S(1)} %slice_reduce_fusion), channel_id=1, source_target_pairs={{0,1},{1,0},{2,3},{3,2},{4,5},{5,4},{6,7},{7,6},{8,9},{9,8},{10,11... | collective-permute-start | bytes 49160 | tf_op jit(solution)/shard_map/ppermute | solution.py:376
  18.2 2.2 %collective-permute-done = f32[16,256]{1,0:T(8,128)S(1)} collective-permute-done((f32[16,256]{1,0:T(8,128)S(1)}, f32[16,256]{1,0:T(8,128)S(1)}, u32[]{:S(2)}, u32[]{:S(2)}) %collective-permute-start) | collective-permute-done | bytes 16416 | tf_op jit(solution)/shard_map/ppermute | solution.py:376
  20.4 2.6 %collective-permute-start.1 = (f32[16,256]{1,0:T(8,128)S(1)}, f32[16,256]{1,0:T(8,128)S(1)}, u32[]{:S(2)}, u32[]{:S(2)}) collective-permute-start(f32[16,256]{1,0:T(8,128)S(1)} %add.6), channel_id=1, source_target_pairs={{0,2},{1,3},{2,0},{3,1},{4,6},{5,7},{6,4},{7,5},{8,10},{9,11},{10,... | collective-permute-start | bytes 49160 | tf_op jit(solution)/shard_map/ppermute | solution.py:376
  22.9 2.0 %collective-permute-done.1 = f32[16,256]{1,0:T(8,128)S(1)} collective-permute-done((f32[16,256]{1,0:T(8,128)S(1)}, f32[16,256]{1,0:T(8,128)S(1)}, u32[]{:S(2)}, u32[]{:S(2)}) %collective-permute-start.1) | collective-permute-done | bytes 16416 | tf_op jit(solution)/shard_map/ppermute | solution.py:376
  25.0 0.6 %add.7.shared = f32[16,256]{1,0:T(8,128)} add(f32[16,256]{1,0:T(8,128)S(1)} %add.6, f32[16,256]{1,0:T(8,128)S(1)} %collective-permute-done.1) | non-fusion elementwise | flops 4096 | bytes 49152 | tf_op jit(solution)/shard_map/add | solution.py:376
  25.6 0.0 copy-done
  25.6 29.0 %panel.1 = (f32[2048,512]{1,0:T(8,128)}, f32[256,256]{1,0:T(8,128)}) custom-call(f32[8,32,256]{2,1,0:T(8,128)} %copy-done, f32[16,256]{1,0:T(8,128)} %add.7.shared, s32[8,8,2]{2,1,0:T(8,128)} %copy.9.table, s32[1,256]{1,0:T(1,128)} %bitcast.7, f32[4,2,512]{2,1,0:T(2,128)} %column_geometry.1, f32[256,256]{1,0:T(8,128)} %lower_inv.1, f32[256,256]{1,0:T(8,128)} %upper_inv.1), custom_call_target="tpu_custom_call" | custom-call | tf_op jit(solution)/shard_map/panel/pallas_call | solution.py:378
  (2 shorter events, 0.0 us)
Async XLA Ops:
  16.5 9.1 %copy-start = (f32[8,32,256]{2,1,0:T(8,128)}, f32[8,32,256]{2,1,0:T(8,128)S(1)}, u32[]{:S(2)}) copy-start(f32[8,32,256]{2,1,0:T(8,128)S(1)} %all_to_all.5.arrived) | copy-start | bytes 786436
  16.5 3.8 %collective-permute-start = (f32[16,256]{1,0:T(8,128)S(1)}, f32[16,256]{1,0:T(8,128)S(1)}, u32[]{:S(2)}, u32[]{:S(2)}) collective-permute-start(f32[16,256]{1,0:T(8,128)S(1)} %slice_reduce_fusion), channel_id=1, source_target_pairs={{0,1},{1,0},{2,3},{3,2},{4,5},{5,4},{6,7},{7,6},{8,9},{9,8},{10,11... | collective-permute-start | bytes 49160 | tf_op jit(solution)/shard_map/ppermute | solution.py:376
  20.4 4.6 %collective-permute-start.1 = (f32[16,256]{1,0:T(8,128)S(1)}, f32[16,256]{1,0:T(8,128)S(1)}, u32[]{:S(2)}, u32[]{:S(2)}) collective-permute-start(f32[16,256]{1,0:T(8,128)S(1)} %add.6), channel_id=1, source_target_pairs={{0,2},{1,3},{2,0},{3,1},{4,6},{5,7},{6,4},{7,5},{8,10},{9,11},{10,... | collective-permute-start | bytes 49160 | tf_op jit(solution)/shard_map/ppermute | solution.py:376
